TPU v7x, 512 devices: a whole 4x8x8 slice. The times are simulated.
512 devices in a mesh: freq: 8 (over z_hi, core), depth: 64 (over z_lo, y, x).
Axes of the slice: x: 4, y: 8, z: 8 (z_hi: 4, z_lo: 2; z = z_hi * 2 + z_lo), core: 2. Of those that a mesh axis runs over, the one named last changes fastest.
Arguments:
- green_source: bfloat16 [16, 64, 384, 2, 256], P('freq', 'depth'), may hold values from -6 to 6
- green_receiver: bfloat16 [16, 64, 128, 2, 256], P('freq', 'depth'), may hold values from -6 to 6
- source_index: int32 [1024], replicated, may hold values from 0 to 383
- receiver_index: int32 [1024], replicated, may hold values from 0 to 127
- frequency_bins: int32 [16], P('freq'), may hold values from 0 to 127
- depth_profile: float32 [64], P('depth'), may hold values from 0.5 to 2
Outputs:
- kernels: float32 [4, 1024, 64], P(None, ('freq', 'depth'))
All inputs are finite; a program needn't handle non-finite values.
Results may differ from a plain program's by a relative error of at most 0.0015.
Values may be sent and summed in bfloat16 or wider, within the bound.
A program may use at most 64 MiB of HBM per device.

v0:
```python
import math

import jax
import jax.numpy as jnp
from jax import lax
from jax.sharding import PartitionSpec as P

NBINS = 128
WX = 16
WY = 16


def extended(block, sides, width):
    for axis, dim in sides:
        count = lax.axis_size(axis)
        forward = [(i, i + 1) for i in range(count - 1)]
        backward = [(target, source) for source, target in forward]
        low = lax.ppermute(
            lax.slice_in_dim(block, block.shape[dim] - width, None, axis=dim), axis, forward
        )
        high = lax.ppermute(lax.slice_in_dim(block, 0, width, axis=dim), axis, backward)
        block = jnp.concatenate([low, block, high], axis=dim)
    return block


def window_slope(values, direction):
    window = values.reshape(values.shape[:-1] + (WX, WY))
    axis_index = window.ndim - 2 + direction
    extent = window.shape[axis_index]
    widths = [(0, 0)] * axis_index + [(1, 1)] + [(0, 0)] * (window.ndim - axis_index - 1)
    padded = jnp.pad(window, widths)
    upper = lax.slice_in_dim(padded, 2, extent + 2, axis=axis_index)
    lower = lax.slice_in_dim(padded, 0, extent, axis=axis_index)
    return (0.5 * (upper - lower)).reshape(values.shape)


def all_pairs(left, right, flat_index):
    full = jnp.einsum("sam,ram->sr", left, right, preferred_element_type=jnp.float32)
    return full.reshape(-1)[flat_index]


def on_device(
    green_source, green_receiver, source_index, receiver_index, frequency_bins, depth_profile
):
    local_freqs, local_depths, sources, _, cells = green_source.shape
    receivers = green_receiver.shape[2]
    pairs = source_index.shape[0]
    n_freq = lax.axis_size("freq")
    scaled_freq = 0.5 + frequency_bins.astype(jnp.float32) / NBINS
    kernel_scale = 1.0 / math.sqrt(2.0 * WX * WY * local_freqs * n_freq)
    flat_index = source_index * receivers + receiver_index
    sign_table = jnp.array([1.0, -1.0], jnp.bfloat16)[:, None]
    swapped = jnp.flip(green_receiver, axis=3)
    signed = green_receiver * sign_table
    wide_source = green_source.astype(jnp.float32)
    slope_x = window_slope(wide_source, 0).astype(jnp.bfloat16)
    slope_y = window_slope(wide_source, 1).astype(jnp.bfloat16)
    padded = extended(green_source, (("depth", 1),), 1)
    total = jnp.zeros((4, pairs), jnp.float32)
    for freq_slot in range(local_freqs):
        plain = all_pairs(green_source[freq_slot, 0], signed[freq_slot, 0], flat_index)
        along_x = all_pairs(slope_x[freq_slot, 0], swapped[freq_slot, 0], flat_index)
        along_y = all_pairs(slope_y[freq_slot, 0], swapped[freq_slot, 0], flat_index)
        upper = all_pairs(padded[freq_slot, 2], swapped[freq_slot, 0], flat_index)
        lower = all_pairs(padded[freq_slot, 0], swapped[freq_slot, 0], flat_index)
        weight = scaled_freq[freq_slot]
        first = plain * (weight * weight) * depth_profile[0]
        fourth = 0.5 * (upper - lower) * weight
        total = total + jnp.stack([first, along_x * weight, along_y * weight, fourth], axis=0)
    columns = [total * kernel_scale]
    partial_value = jnp.stack(columns, axis=-1)
    summed = lax.psum_scatter(partial_value, "freq", scatter_dimension=1, tiled=True)
    pair_tiles = lax.all_to_all(summed, "depth", split_axis=1, concat_axis=2, tiled=True)
    return pair_tiles


def solution(mesh):
    placed = (
        P("freq", "depth", None, None, None),
        P("freq", "depth", None, None, None),
        P(),
        P(),
        P("freq"),
        P("depth"),
    )
    return jax.shard_map(
        on_device,
        mesh=mesh,
        in_specs=placed,
        out_specs=P(None, ("freq", "depth"), None),
        check_vma=False,
    )
```

profile of v0, /device:TPU:1, one launch (start us, length us, event | category | flops | bytes accessed | tf_op | source)
XLA Modules:
  0.0 171.6 jit_solution(5848652722109166681)
XLA Ops:
  6.5 1.3 copy.68
  7.9 1.3 collective-permute-start
  9.2 5.5 %collective-permute-start.1 = (bf16[2,1,384,2,256]{4,2,3,1,0:T(8,128)(2,1)S(1)}, bf16[2,1,384,2,256]{4,2,3,1,0:T(8,128)(2,1)}, u32[]{:S(2)}, u32[]{:S(2)}) collective-permute-start(bf16[2,1,384,2,256]{4,2,3,1,0:T(8,128)(2,1)S(1)} %copy.68), channel_id=1, source_target_pairs={{0,1},{1,2},{2,3},{3,4},{4,5},{5,6},{6,7},{7,8},{8,9},{9,10},{10,1... | collective-permute-start | bytes 2359304 | tf_op jit(solution)/shard_map/ppermute | solution.py:18
  14.7 0.6 copy.70
  15.3 0.6 fusion.19
  20.2 0.7 slice.94
  20.9 0.7 slice.83
  21.7 0.6 fusion.2
  22.8 0.3 convolution_bitcast_fusion.2
  23.2 6.2 %gather_fusion.6 = f32[1024]{0:T(1024)S(1)} fusion(f32[49152]{0:T(1024)S(1)} %convolution_bitcast_fusion.3, s32[1024]{0:T(1024)S(1)} %fusion.15), kind=kCustom, calls=%fused_computation.6 | custom fusion | bytes 12288 | tf_op jit(solution)/shard_map/gather | solution.py:39
  29.3 6.2 %gather_fusion.7 = f32[1024]{0:T(1024)S(1)} fusion(f32[49152]{0:T(1024)S(1)} %convolution_bitcast_fusion.2, s32[1024]{0:T(1024)S(1)} %fusion.15), kind=kCustom, calls=%fused_computation.7 | custom fusion | bytes 12288 | tf_op jit(solution)/shard_map/gather | solution.py:39
  35.8 6.2 %gather_fusion.1 = f32[1024]{0:T(1024)S(1)} fusion(f32[49152]{0:T(1024)S(1)} %convolution_bitcast_fusion.7, s32[1024]{0:T(1024)S(1)} %fusion.15), kind=kCustom, calls=%fused_computation.1 | custom fusion | bytes 12288 | tf_op jit(solution)/shard_map/gather | solution.py:39
  42.3 6.2 %gather_fusion.2 = f32[1024]{0:T(1024)S(1)} fusion(f32[49152]{0:T(1024)S(1)} %convolution_bitcast_fusion.6, s32[1024]{0:T(1024)S(1)} %fusion.15), kind=kCustom, calls=%fused_computation.2 | custom fusion | bytes 12288 | tf_op jit(solution)/shard_map/gather | solution.py:39
  49.0 6.2 %gather_fusion = f32[1024]{0:T(1024)S(1)} fusion(f32[49152]{0:T(1024)S(1)} %bitcast.100, s32[1024]{0:T(1024)S(1)} %fusion.15), kind=kCustom, calls=%fused_computation | custom fusion | bytes 12288 | tf_op jit(solution)/shard_map/gather | solution.py:39
  55.5 6.2 %gather_fusion.5 = f32[1024]{0:T(1024)S(1)} fusion(f32[49152]{0:T(1024)S(1)} %bitcast.101, s32[1024]{0:T(1024)S(1)} %fusion.15), kind=kCustom, calls=%fused_computation.5 | custom fusion | bytes 12288 | tf_op jit(solution)/shard_map/gather | solution.py:39
  62.3 0.7 broadcast_multiply_fusion
  63.0 0.7 broadcast_multiply_fusion.2
  63.7 1.3 convolution_bitcast_fusion.1
  65.0 6.2 %gather_fusion.8 = f32[1024]{0:T(1024)S(1)} fusion(f32[49152]{0:T(1024)S(1)} %convolution_bitcast_fusion.1, s32[1024]{0:T(1024)S(1)} %fusion.15), kind=kCustom, calls=%fused_computation.8 | custom fusion | bytes 12288 | tf_op jit(solution)/shard_map/gather | solution.py:39
  71.2 1.3 convolution_bitcast_fusion
  72.4 6.2 %gather_fusion.9 = f32[1024]{0:T(1024)S(1)} fusion(f32[49152]{0:T(1024)S(1)} %convolution_bitcast_fusion, s32[1024]{0:T(1024)S(1)} %fusion.15), kind=kCustom, calls=%fused_computation.9 | custom fusion | bytes 12288 | tf_op jit(solution)/shard_map/gather | solution.py:39
  78.6 1.3 convolution_bitcast_fusion.5
  79.9 6.2 %gather_fusion.3 = f32[1024]{0:T(1024)S(1)} fusion(f32[49152]{0:T(1024)S(1)} %convolution_bitcast_fusion.5, s32[1024]{0:T(1024)S(1)} %fusion.15), kind=kCustom, calls=%fused_computation.3 | custom fusion | bytes 12288 | tf_op jit(solution)/shard_map/gather | solution.py:39
  86.0 1.3 convolution_bitcast_fusion.4
  87.3 6.2 %gather_fusion.4 = f32[1024]{0:T(1024)S(1)} fusion(f32[49152]{0:T(1024)S(1)} %convolution_bitcast_fusion.4, s32[1024]{0:T(1024)S(1)} %fusion.15), kind=kCustom, calls=%fused_computation.4 | custom fusion | bytes 12288 | tf_op jit(solution)/shard_map/gather | solution.py:39
  93.5 0.9 copy.93
  94.4 2.0 %bitcast_reduce_fusion = f32[1024,4]{1,0:T(8,128)} fusion(f32[4,1024,1]{2,0,1:T(4,128)S(1)} %copy.93), kind=kLoop, calls=%fused_computation.20 | loop fusion | bytes 32768
  96.4 46.1 %reduce-scatter.4.cloned.1.call-done = f32[128,4]{1,0:T(8,128)} async-done(((f32[1024,4]{1,0:T(8,128)}), f32[128,4]{1,0:T(8,128)}) %reduce-scatter.4.cloned.1.call-update) | async-done | bytes 2064
  142.5 1.0 reshape_bitcast_fusion
  143.5 0.9 copy.87
  144.4 19.6 %all_to_all.18 = f32[4,128,1]{0,2,1:T(1,128)S(1)} all-to-all(f32[4,128,1]{0,2,1:T(1,128)S(1)} %copy.87), channel_id=1, replica_groups=mesh['freq'=8,'depth'=64] {'depth'}, dimensions={1} | all-to-all | bytes 4096 | tf_op jit(solution)/shard_map/all_to_all | solution.py:73
  164.0 0.7 copy.88
  (34 shorter events, 2.4 us)
Async XLA Ops:
  6.5 8.1 %copy-start = (bf16[2,1,384,2,256]{4,3,2,1,0:T(2,128)(2,1)S(1)}, bf16[2,1,384,2,256]{4,3,2,1,0:T(2,128)(2,1)}, u32[]{:S(2)}) copy-start(bf16[2,1,384,2,256]{4,3,2,1,0:T(2,128)(2,1)} %param.7) | copy-start | bytes 2359300
  6.5 8.8 %copy-start.5 = (s32[2]{0:T(128)S(1)}, s32[2]{0:T(128)}, u32[]{:S(2)}) copy-start(s32[2]{0:T(128)} %param.11) | copy-start | bytes 28
  6.5 13.4 %copy-start.1 = (bf16[2,1,128,2,256]{4,3,2,1,0:T(2,128)(2,1)S(1)}, bf16[2,1,128,2,256]{4,3,2,1,0:T(2,128)(2,1)}, u32[]{:S(2)}) copy-start(bf16[2,1,128,2,256]{4,3,2,1,0:T(2,128)(2,1)} %param.8) | copy-start | bytes 786436
  6.5 136.0 %reduce-scatter.4.cloned.1.call-start = ((), (), s32[]{:S(2)}) async-start(), calls=%async_computation.2 | async-start | bytes 589824
  7.9 55.9 %collective-permute-start = (bf16[2,1,384,2,256]{4,2,3,1,0:T(8,128)(2,1)S(1)}, bf16[2,1,384,2,256]{4,2,3,1,0:T(8,128)(2,1)}, u32[]{:S(2)}, u32[]{:S(2)}) collective-permute-start(bf16[2,1,384,2,256]{4,2,3,1,0:T(8,128)(2,1)S(1)} %copy.68), channel_id=1, source_target_pairs={{1,0},{2,1},{3,2},{4,3},{5,4},{6,5},{7,6},{8,7},{9,8},{10,9},{11,1... | collective-permute-start | bytes 2359304 | tf_op jit(solution)/shard_map/ppermute | solution.py:21
  9.2 62.0 %collective-permute-start.1 = (bf16[2,1,384,2,256]{4,2,3,1,0:T(8,128)(2,1)S(1)}, bf16[2,1,384,2,256]{4,2,3,1,0:T(8,128)(2,1)}, u32[]{:S(2)}, u32[]{:S(2)}) collective-permute-start(bf16[2,1,384,2,256]{4,2,3,1,0:T(8,128)(2,1)S(1)} %copy.68), channel_id=1, source_target_pairs={{0,1},{1,2},{2,3},{3,4},{4,5},{5,6},{6,7},{7,8},{8,9},{9,10},{10,1... | collective-permute-start | bytes 2359304 | tf_op jit(solution)/shard_map/ppermute | solution.py:18
  22.4 0.7 copy-start.2
  22.4 0.7 copy-start.3
  42.3 6.2 %copy-start.4 = (bf16[2]{0:T(256)(128)(2,1)S(1)}, bf16[2]{0:T(256)(128)(2,1)}, u32[]{:S(2)}) copy-start(bf16[2]{0:T(256)(128)(2,1)} %constant.20.clone) | copy-start | bytes 16
Sparse Core Ops, SparseCore 0:
  96.5 45.9 reduce-scatter.3
where the time goes:
time: 173 us; the launch traced here: 172 us
  local copies, waits for them, and re-layouts  71.6 us (41%)
  waiting for transfers between devices  46.1 us (27%)
  blocking collectives  19.6 us (11%)
  between operations  18.4 us (11%)
  matrix products  6.79 us (4%)
  starting transfers between devices  6.78 us (4%)
  other arithmetic  2.21 us (1%)
    gather x10, local copies, waits for them, and re-layouts, all_pairs(): return full.reshape(-1)[flat_index]  61.5 us
    unnamed x2, waiting for transfers between devices  46.1 us
    all_to_all x1, blocking collectives, on_device(): lax.all_to_all(summed, 'depth', split_axis=1, concat_axis=2, tiled=True)  19.6 us
    dot_general x10, matrix products, all_pairs(): jnp.einsum('sam,ram->sr', left, right, preferred_element_type=jnp.float32)  6.79 us
    unnamed x17, local copies, waits for them, and re-layouts  5.87 us
    ppermute x1, starting transfers between devices, extended(): lax.ppermute(lax.slice_in_dim(block, block.shape[dim] - width, None, axis...  5.49 us
  transfers between devices with their start and end apart: 3, of which 1 were waited for; matrix products, arithmetic and copies ran while one was open for 30% of the time, Pallas kernels for 0%

commit v1 on v0

v1 whole, which is shorter than its diff:
```python
import functools
import math

import jax
import jax.numpy as jnp
from jax import lax
from jax.experimental import pallas as pl
from jax.experimental.pallas import tpu as pltpu
from jax.sharding import PartitionSpec as P

NBINS = 128
WX = 16
WY = 16
CELLS = WX * WY
ZL = 2
LANES = 128
CHANNELS = 8
MESH = pl.DeviceIdType.MESH


def contract_cells(left, right):
    return lax.dot_general(
        left, right, (((1,), (1,)), ((), ())), preferred_element_type=jnp.float32
    )


def split_parts(value):
    high = value.astype(jnp.bfloat16)
    low = (value - high.astype(jnp.float32)).astype(jnp.bfloat16)
    return high, low


def adjoint_slopes(block):
    wide = block.astype(jnp.float32)
    cell = lax.broadcasted_iota(jnp.int32, wide.shape, 1)
    column = lax.rem(cell, WY)
    before_x = jnp.where(cell >= WY, pltpu.roll(wide, WY, 1), 0.0)
    after_x = jnp.where(cell < CELLS - WY, pltpu.roll(wide, CELLS - WY, 1), 0.0)
    before_y = jnp.where(column >= 1, pltpu.roll(wide, 1, 1), 0.0)
    after_y = jnp.where(column < WY - 1, pltpu.roll(wide, CELLS - 1, 1), 0.0)
    return split_parts(0.5 * (before_x - after_x)) + split_parts(0.5 * (before_y - after_y))


def kernel(
    n_freq, n_depth, scale,
    src, rec, sidx, ridx, bins, profile, out,
    near, onehot, terms, sbuf1, rbuf1, square1, sbuf2, rbuf2, square2,
    near_send, near_recv, send1, recv1, send2, recv2,
):
    f = lax.axis_index("freq")
    d = lax.axis_index("depth")
    group = n_freq * ZL
    plane = n_depth // ZL
    zl = d // plane
    q = d % plane
    g = f * ZL + zl
    slots, _, receivers, _ = rec.shape
    sources = src.shape[2]
    pairs = sidx.shape[1]
    part = pairs // group
    chunk = min(256, pairs)
    above = (d + 1) % n_depth
    below = (d + n_depth - 1) % n_depth

    barrier = pltpu.get_barrier_semaphore()

    def column_device(member):
        return (member // ZL, (member % ZL) * plane + q)

    def plane_device(member):
        return (f, zl * plane + member)

    for target in (above, below):
        pl.semaphore_signal(barrier, inc=1, device_id=(f, target), device_id_type=MESH)

    @pl.loop(1, group)
    def _(step):
        pl.semaphore_signal(
            barrier, inc=1, device_id=column_device((g + step) % group), device_id_type=MESH
        )

    @pl.loop(1, plane)
    def _(step):
        pl.semaphore_signal(
            barrier, inc=1, device_id=plane_device((q + step) % plane), device_id_type=MESH
        )

    pl.semaphore_wait(barrier, 2 + group - 1 + plane - 1)

    near_copies = []
    for slot in range(slots):
        for side, target in enumerate((above, below)):
            copy = pltpu.make_async_remote_copy(
                src_ref=rec.at[slot],
                dst_ref=near.at[side, slot],
                send_sem=near_send.at[side, slot],
                recv_sem=near_recv.at[side, slot],
                device_id=(f, target),
                device_id_type=MESH,
            )
            copy.start()
            near_copies.append(copy)

    source_rows = lax.broadcasted_iota(jnp.int32, (sources, pairs), 0)
    onehot[...] = jnp.where(source_rows == sidx[...], 1.0, 0.0).astype(jnp.bfloat16)
    terms[...] = jnp.zeros_like(terms)
    square1[...] = jnp.zeros_like(square1)
    square2[...] = jnp.zeros_like(square2)

    def pick(full, first):
        high, low = split_parts(full)
        count = full.shape[0] // receivers
        for start in range(0, pairs, chunk):
            hot = onehot[:, start : start + chunk]
            rows = jnp.dot(high, hot, preferred_element_type=jnp.float32) + jnp.dot(
                low, hot, preferred_element_type=jnp.float32
            )
            wanted = (
                lax.broadcasted_iota(jnp.int32, (receivers, chunk), 0)
                == ridx[:, start : start + chunk]
            )
            for channel in range(count):
                block = rows[channel * receivers : (channel + 1) * receivers]
                terms[first + channel : first + channel + 1, start : start + chunk] = jnp.sum(
                    jnp.where(wanted, block, 0.0), axis=0, keepdims=True
                )

    weights = [0.5 + bins[slot].astype(jnp.float32) * (1.0 / NBINS) for slot in range(slots)]
    own = None
    for slot in range(slots):
        r_re = rec[slot, 0]
        r_im = rec[slot, 1]
        left_re = jnp.concatenate((r_re,) + adjoint_slopes(r_im), axis=0)
        left_im = jnp.concatenate((-r_im,) + adjoint_slopes(r_re), axis=0)
        full = contract_cells(left_re, src[slot, 0]) + contract_cells(left_im, src[slot, 1])
        parts = [full[i * receivers : (i + 1) * receivers] for i in range(5)]
        weight = weights[slot]
        first = parts[0] * (weight * weight * profile[0] * scale)
        second = (parts[1] + parts[2]) * (weight * scale)
        third = (parts[3] + parts[4]) * (weight * scale)
        fresh = jnp.concatenate([first, second, third], axis=0)
        own = fresh if own is None else own + fresh
    pick(own, 0)

    beside = None
    for slot in range(slots):
        for side in range(2):
            near_copies[slot * 2 + side].wait_recv()
        left_re = jnp.concatenate([near[0, slot, 1], near[1, slot, 1]], axis=0)
        left_im = jnp.concatenate([near[0, slot, 0], near[1, slot, 0]], axis=0)
        full = contract_cells(left_re, src[slot, 0]) + contract_cells(left_im, src[slot, 1])
        fresh = full * (0.5 * weights[slot] * scale)
        beside = fresh if beside is None else beside + fresh
    pick(beside, 3)

    for member in range(group):
        sbuf1[member, :, 0:part] = terms[:, member * part : (member + 1) * part]

    def copy1(step):
        member = (g + step) % group
        return pltpu.make_async_remote_copy(
            src_ref=sbuf1.at[member],
            dst_ref=rbuf1.at[g],
            send_sem=send1.at[member],
            recv_sem=recv1.at[g],
            device_id=column_device(member),
            device_id_type=MESH,
        )

    def arrived1(step):
        member = (g + step) % group
        return pltpu.make_async_remote_copy(
            src_ref=sbuf1.at[member],
            dst_ref=rbuf1.at[member],
            send_sem=send1.at[member],
            recv_sem=recv1.at[member],
            device_id=column_device(member),
            device_id_type=MESH,
        )

    @pl.loop(1, group)
    def _(step):
        copy1(step).start()

    rbuf1[g] = sbuf1[g]

    @pl.loop(1, group)
    def _(step):
        arrived1(step).wait_recv()

    for low in range(ZL):
        total = rbuf1[low, :, 0:part]
        for member in range(1, n_freq):
            total = total + rbuf1[member * ZL + low, :, 0:part]
        square1[low * CHANNELS : (low + 1) * CHANNELS, 0:part] = total
    turned = square1[...].T
    for member in range(plane):
        sbuf2[member] = turned[2 * member : 2 * member + 2]

    def copy2(step):
        member = (q + step) % plane
        return pltpu.make_async_remote_copy(
            src_ref=sbuf2.at[member],
            dst_ref=rbuf2.at[q],
            send_sem=send2.at[member],
            recv_sem=recv2.at[q],
            device_id=plane_device(member),
            device_id_type=MESH,
        )

    def arrived2(step):
        member = (q + step) % plane
        return pltpu.make_async_remote_copy(
            src_ref=sbuf2.at[member],
            dst_ref=rbuf2.at[member],
            send_sem=send2.at[member],
            recv_sem=recv2.at[member],
            device_id=plane_device(member),
            device_id_type=MESH,
        )

    @pl.loop(1, plane)
    def _(step):
        copy2(step).start()

    rbuf2[q] = sbuf2[q]

    @pl.loop(1, plane)
    def _(step):
        arrived2(step).wait_recv()

    for owned in range(2):
        square2[owned * plane : (owned + 1) * plane, :] = rbuf2[:, owned, :]
    columns = square2[...].T
    gap = jnp.zeros((1, 1), jnp.float32)
    for owned in range(2):
        spread = slice(owned * plane, (owned + 1) * plane)
        depths = jnp.concatenate(
            [columns[low * CHANNELS : (low + 1) * CHANNELS, spread] for low in range(ZL)], axis=1
        )
        for channel in range(3):
            out[channel, owned : owned + 1, :] = depths[channel : channel + 1]
        upper = jnp.concatenate([depths[3:4, 1:], gap], axis=1)
        lower = jnp.concatenate([gap, depths[4:5, :-1]], axis=1)
        out[3, owned : owned + 1, :] = upper - lower

    for copy in near_copies:
        copy.wait_send()

    @pl.loop(1, group)
    def _(step):
        copy1(step).wait_send()

    @pl.loop(1, plane)
    def _(step):
        copy2(step).wait_send()


def on_device(
    green_source, green_receiver, source_index, receiver_index, frequency_bins, depth_profile
):
    slots, _, sources, _, cells = green_source.shape
    receivers = green_receiver.shape[2]
    pairs = source_index.shape[0]
    n_freq = lax.axis_size("freq")
    n_depth = lax.axis_size("depth")
    group = n_freq * ZL
    plane = n_depth // ZL
    scale = 1.0 / math.sqrt(2.0 * WX * WY * slots * n_freq)
    src = jnp.transpose(green_source[:, 0], (0, 2, 1, 3))
    rec = jnp.transpose(green_receiver[:, 0], (0, 2, 1, 3))
    vmem = pl.BlockSpec(memory_space=pltpu.VMEM)
    smem = pl.BlockSpec(memory_space=pltpu.SMEM)
    return pl.pallas_call(
        functools.partial(kernel, n_freq, n_depth, scale),
        out_shape=jax.ShapeDtypeStruct((4, pairs // (n_freq * n_depth), n_depth), jnp.float32),
        in_specs=[vmem, vmem, vmem, vmem, smem, smem],
        out_specs=vmem,
        scratch_shapes=[
            pltpu.VMEM((2, slots, 2, receivers, cells), jnp.bfloat16),
            pltpu.VMEM((sources, pairs), jnp.bfloat16),
            pltpu.VMEM((CHANNELS, pairs), jnp.float32),
            pltpu.VMEM((group, CHANNELS, LANES), jnp.float32),
            pltpu.VMEM((group, CHANNELS, LANES), jnp.float32),
            pltpu.VMEM((LANES, LANES), jnp.float32),
            pltpu.VMEM((plane, 2, LANES), jnp.float32),
            pltpu.VMEM((plane, 2, LANES), jnp.float32),
            pltpu.VMEM((LANES, LANES), jnp.float32),
            pltpu.SemaphoreType.DMA((2, slots)),
            pltpu.SemaphoreType.DMA((2, slots)),
            pltpu.SemaphoreType.DMA((group,)),
            pltpu.SemaphoreType.DMA((group,)),
            pltpu.SemaphoreType.DMA((plane,)),
            pltpu.SemaphoreType.DMA((plane,)),
        ],
        compiler_params=pltpu.CompilerParams(collective_id=0, has_side_effects=True),
    )(
        src,
        rec,
        source_index.reshape(1, pairs),
        receiver_index.reshape(1, pairs),
        frequency_bins,
        depth_profile,
    )


def solution(mesh):
    placed = (
        P("freq", "depth", None, None, None),
        P("freq", "depth", None, None, None),
        P(),
        P(),
        P("freq"),
        P("depth"),
    )
    return jax.shard_map(
        on_device,
        mesh=mesh,
        in_specs=placed,
        out_specs=P(None, ("freq", "depth"), None),
        check_vma=False,
    )
```

time: 173 us -> 45.3 us (0.26)
  local copies, waits for them, and re-layouts: 71.6 us -> 5.07 us
  waiting for transfers between devices: 46.1 us -> 0 us
  Pallas kernels: 0 us -> 39.3 us
  blocking collectives: 19.6 us -> 0 us
  between operations: 18.4 us -> 0.66 us
  matrix products: 6.79 us -> 0 us
  starting transfers between devices: 6.78 us -> 0 us
  other arithmetic: 2.21 us -> 0 us
    gather x10 -> x0, local copies, waits for them, and re-layouts: 61.5 us -> none  [all_pairs(): return full.reshape(-1)[flat_index]]
    unnamed x2 -> x0, waiting for transfers between devices: 46.1 us -> none
    pallas_call x0 -> x1, Pallas kernels: none -> 39.3 us  [on_device(): pl.pallas_call(functools.partial(kernel, n_freq, n_depth, scale), out_sha...]
    all_to_all x1 -> x0, blocking collectives: 19.6 us -> none  [on_device(): lax.all_to_all(summed, 'depth', split_axis=1, concat_axis=2, tiled=True)]
    dot_general x10 -> x0, matrix products: 6.79 us -> none  [all_pairs(): jnp.einsum('sam,ram->sr', left, right, preferred_element_type=jnp.float32)]
    ppermute x2 -> x0, starting transfers between devices: 6.78 us -> none  [the longest x1 5.49 us: extended(): lax.ppermute(lax.slice_in_dim(block, block.shape[dim] - width, None, axis...]
    slice x6 -> x0, local copies, waits for them, and re-layouts: 2.38 us -> none  [the longest x3 1.62 us: on_device(): swapped[freq_slot, 0]]
    unnamed x17 -> x3, local copies, waits for them, and re-layouts: 5.87 us -> 5.07 us
  transfers between devices with their start and end apart: 3 -> 0, of which waited for: 1 -> 0; matrix products, arithmetic and copies ran while one was open for 30% -> 0% of each run, Pallas kernels for 0% -> 0%
where the time goes in v1:
time: 45.3 us; the launch traced here: 45 us
  Pallas kernels  39.3 us (87%)
  local copies, waits for them, and re-layouts  5.07 us (11%)
  between operations  0.66 us (1%)
    pallas_call x1, Pallas kernels, on_device(): pl.pallas_call(functools.partial(kernel, n_freq, n_depth, scale), out_sha...  39.3 us
    unnamed x3, local copies, waits for them, and re-layouts  5.07 us

profile of v1, /device:TPU:1, one launch (start us, length us, event | category | flops | bytes accessed | tf_op | source)
XLA Modules:
  0.0 45.0 jit_solution(17741959811199991868)
XLA Ops:
  0.7 1.7 %copy.12 = bf16[2,1,128,2,256]{4,2,3,0,1:T(8,128)(2,1)} copy(bf16[2,1,128,2,256]{4,3,2,1,0:T(2,128)(2,1)} %param.7) | data formatting | bytes 524288 | tf_op args[1]
  2.3 2.1 %copy.11 = bf16[2,1,384,2,256]{4,2,3,0,1:T(8,128)(2,1)} copy(bf16[2,1,384,2,256]{4,3,2,1,0:T(2,128)(2,1)} %param.6) | data formatting | bytes 1572864 | tf_op args[0]
  4.5 39.3 %shard_map.64 = f32[4,2,64]{2,1,0:T(2,128)} custom-call(bf16[2,2,384,256]{3,2,1,0:T(8,128)(2,1)} %bitcast.12, bf16[2,2,128,256]{3,2,1,0:T(8,128)(2,1)} %bitcast.13, s32[1,1024]{1,0:T(1,128)} %bitcast.14, s32[1,1024]{1,0:T(1,128)} %bitcast.15, s32[2]{0:T(128)} %bins.1, f32[1]{0:T(128)S(6)} %copy.14.profile), custom_call_target="tpu_custom_call" | custom-call | tf_op jit(solution)/shard_map/pallas_call | solution.py:274
  43.8 1.3 %copy.15 = f32[4,2,64]{2,1,0:T(2,128)} copy(f32[4,2,64]{2,1,0:T(2,128)} %shard_map.64) | data formatting | bytes 4096

commit v2 on v1

--- a/solution.py
+++ b/solution.py
@@ -43,9 +43,9 @@
 
 def kernel(
     n_freq, n_depth, scale,
-    src, rec, sidx, ridx, bins, profile, out,
-    near, onehot, terms, sbuf1, rbuf1, square1, sbuf2, rbuf2, square2,
-    near_send, near_recv, send1, recv1, send2, recv2,
+    source, receiver, sidx, ridx, bins, profile, out,
+    src_raw, rec_raw, src, rec, near, onehot, terms, sbuf1, rbuf1, square1, sbuf2, rbuf2, square2,
+    fetch, near_send, near_recv, send1, recv1, send2, recv2,
 ):
     f = lax.axis_index("freq")
     d = lax.axis_index("depth")
@@ -62,6 +62,10 @@
     above = (d + 1) % n_depth
     below = (d + n_depth - 1) % n_depth
 
+    fetch_rec = pltpu.make_async_copy(receiver, rec_raw, fetch.at[0])
+    fetch_src = pltpu.make_async_copy(source, src_raw, fetch.at[1])
+    fetch_rec.start()
+    fetch_src.start()
     barrier = pltpu.get_barrier_semaphore()
 
     def column_device(member):
@@ -85,6 +89,19 @@
             barrier, inc=1, device_id=plane_device((q + step) % plane), device_id_type=MESH
         )
 
+    fetch_rec.wait()
+    for slot in range(slots):
+        for side in range(2):
+            rec[slot, side] = rec_raw[slot, 0, :, side, :]
+    fetch_src.wait()
+    for slot in range(slots):
+        for side in range(2):
+            src[slot, side] = src_raw[slot, 0, :, side, :]
+    source_rows = lax.broadcasted_iota(jnp.int32, (sources, pairs), 0)
+    onehot[...] = jnp.where(source_rows == sidx[...], 1.0, 0.0).astype(jnp.bfloat16)
+    terms[...] = jnp.zeros_like(terms)
+    square1[...] = jnp.zeros_like(square1)
+    square2[...] = jnp.zeros_like(square2)
     pl.semaphore_wait(barrier, 2 + group - 1 + plane - 1)
 
     near_copies = []
@@ -100,12 +117,6 @@
             )
             copy.start()
             near_copies.append(copy)
-
-    source_rows = lax.broadcasted_iota(jnp.int32, (sources, pairs), 0)
-    onehot[...] = jnp.where(source_rows == sidx[...], 1.0, 0.0).astype(jnp.bfloat16)
-    terms[...] = jnp.zeros_like(terms)
-    square1[...] = jnp.zeros_like(square1)
-    square2[...] = jnp.zeros_like(square2)
 
     def pick(full, first):
         high, low = split_parts(full)
@@ -154,7 +165,12 @@
     pick(beside, 3)
 
     for member in range(group):
-        sbuf1[member, :, 0:part] = terms[:, member * part : (member + 1) * part]
+        pair_slice = slice(member * part, (member + 1) * part)
+        for channel in range(5):
+            row, lane = channel // 2, (channel % 2) * part
+            sbuf1[member, row : row + 1, lane : lane + part] = terms[
+                channel : channel + 1, pair_slice
+            ]
 
     def copy1(step):
         member = (g + step) % group
@@ -189,10 +205,13 @@
         arrived1(step).wait_recv()
 
     for low in range(ZL):
-        total = rbuf1[low, :, 0:part]
+        total = rbuf1[low]
         for member in range(1, n_freq):
-            total = total + rbuf1[member * ZL + low, :, 0:part]
-        square1[low * CHANNELS : (low + 1) * CHANNELS, 0:part] = total
+            total = total + rbuf1[member * ZL + low]
+        for channel in range(5):
+            row, lane = channel // 2, (channel % 2) * part
+            target = low * CHANNELS + channel
+            square1[target : target + 1, 0:part] = total[row : row + 1, lane : lane + part]
     turned = square1[...].T
     for member in range(plane):
         sbuf2[member] = turned[2 * member : 2 * member + 2]
@@ -267,25 +286,29 @@
     group = n_freq * ZL
     plane = n_depth // ZL
     scale = 1.0 / math.sqrt(2.0 * WX * WY * slots * n_freq)
-    src = jnp.transpose(green_source[:, 0], (0, 2, 1, 3))
-    rec = jnp.transpose(green_receiver[:, 0], (0, 2, 1, 3))
     vmem = pl.BlockSpec(memory_space=pltpu.VMEM)
+    anywhere = pl.BlockSpec(memory_space=pl.ANY)
     smem = pl.BlockSpec(memory_space=pltpu.SMEM)
     return pl.pallas_call(
         functools.partial(kernel, n_freq, n_depth, scale),
         out_shape=jax.ShapeDtypeStruct((4, pairs // (n_freq * n_depth), n_depth), jnp.float32),
-        in_specs=[vmem, vmem, vmem, vmem, smem, smem],
+        in_specs=[anywhere, anywhere, vmem, vmem, smem, smem],
         out_specs=vmem,
         scratch_shapes=[
+            pltpu.VMEM(green_source.shape, jnp.bfloat16),
+            pltpu.VMEM(green_receiver.shape, jnp.bfloat16),
+            pltpu.VMEM((slots, 2, sources, cells), jnp.bfloat16),
+            pltpu.VMEM((slots, 2, receivers, cells), jnp.bfloat16),
             pltpu.VMEM((2, slots, 2, receivers, cells), jnp.bfloat16),
             pltpu.VMEM((sources, pairs), jnp.bfloat16),
             pltpu.VMEM((CHANNELS, pairs), jnp.float32),
-            pltpu.VMEM((group, CHANNELS, LANES), jnp.float32),
-            pltpu.VMEM((group, CHANNELS, LANES), jnp.float32),
+            pltpu.VMEM((group, 4, LANES), jnp.float32),
+            pltpu.VMEM((group, 4, LANES), jnp.float32),
             pltpu.VMEM((LANES, LANES), jnp.float32),
             pltpu.VMEM((plane, 2, LANES), jnp.float32),
             pltpu.VMEM((plane, 2, LANES), jnp.float32),
             pltpu.VMEM((LANES, LANES), jnp.float32),
+            pltpu.SemaphoreType.DMA((2,)),
             pltpu.SemaphoreType.DMA((2, slots)),
             pltpu.SemaphoreType.DMA((2, slots)),
             pltpu.SemaphoreType.DMA((group,)),
@@ -295,8 +318,8 @@
         ],
         compiler_params=pltpu.CompilerParams(collective_id=0, has_side_effects=True),
     )(
-        src,
-        rec,
+        green_source,
+        green_receiver,
         source_index.reshape(1, pairs),
         receiver_index.reshape(1, pairs),
         frequency_bins,

time: 45.3 us -> 40.8 us (0.901)
  local copies, waits for them, and re-layouts: 5.07 us -> 1.28 us
  Pallas kernels: 39.3 us -> 38.7 us
    unnamed x3 -> x1, local copies, waits for them, and re-layouts: 5.07 us -> 1.28 us
    pallas_call x1, Pallas kernels: 39.3 us -> 38.7 us  [on_device(): pl.pallas_call(functools.partial(kernel, n_freq, n_depth, scale), out_sha...]
where the time goes in v2:
time: 40.8 us; the launch traced here: 40.6 us
  Pallas kernels  38.7 us (95%)
  local copies, waits for them, and re-layouts  1.28 us (3%)
  between operations  0.66 us (2%)
    pallas_call x1, Pallas kernels, on_device(): pl.pallas_call(functools.partial(kernel, n_freq, n_depth, scale), out_sha...  38.7 us
    unnamed x1, local copies, waits for them, and re-layouts  1.28 us

profile of v2, /device:TPU:1, one launch (start us, length us, event | category | flops | bytes accessed | tf_op | source)
XLA Modules:
  0.0 40.6 jit_solution(12889089896199575341)
XLA Ops:
  0.7 38.7 %shard_map.64 = f32[4,2,64]{2,1,0:T(2,128)} custom-call(bf16[2,1,384,2,256]{4,3,2,1,0:T(2,128)(2,1)} %source.1, bf16[2,1,128,2,256]{4,3,2,1,0:T(2,128)(2,1)} %receiver.1, s32[1,1024]{1,0:T(1,128)} %bitcast.2, s32[1,1024]{1,0:T(1,128)} %bitcast.3, s32[2]{0:T(128)} %bins.1, f32[1]{0:T(128)S(6)} %copy.8.profile), custom_call_target="tpu_custom_call" | custom-call | tf_op jit(solution)/shard_map/pallas_call | solution.py:292
  39.4 1.3 %copy.9 = f32[4,2,64]{2,1,0:T(2,128)} copy(f32[4,2,64]{2,1,0:T(2,128)} %shard_map.64) | data formatting | bytes 4096

commit v3 on v2

--- a/solution.py
+++ b/solution.py
@@ -106,17 +106,18 @@
 
     near_copies = []
     for slot in range(slots):
-        for side, target in enumerate((above, below)):
-            copy = pltpu.make_async_remote_copy(
-                src_ref=rec.at[slot],
-                dst_ref=near.at[side, slot],
-                send_sem=near_send.at[side, slot],
-                recv_sem=near_recv.at[side, slot],
-                device_id=(f, target),
-                device_id_type=MESH,
-            )
-            copy.start()
-            near_copies.append(copy)
+        for half in range(2):
+            for side, target in enumerate((above, below)):
+                copy = pltpu.make_async_remote_copy(
+                    src_ref=rec.at[slot, half],
+                    dst_ref=near.at[side, slot, half],
+                    send_sem=near_send.at[side, slot, half],
+                    recv_sem=near_recv.at[side, slot, half],
+                    device_id=(f, target),
+                    device_id_type=MESH,
+                )
+                copy.start()
+                near_copies.append(copy)
 
     def pick(full, first):
         high, low = split_parts(full)
@@ -155,8 +156,8 @@
 
     beside = None
     for slot in range(slots):
-        for side in range(2):
-            near_copies[slot * 2 + side].wait_recv()
+        for index in range(slot * 4, slot * 4 + 4):
+            near_copies[index].wait_recv()
         left_re = jnp.concatenate([near[0, slot, 1], near[1, slot, 1]], axis=0)
         left_im = jnp.concatenate([near[0, slot, 0], near[1, slot, 0]], axis=0)
         full = contract_cells(left_re, src[slot, 0]) + contract_cells(left_im, src[slot, 1])
@@ -309,8 +310,8 @@
             pltpu.VMEM((plane, 2, LANES), jnp.float32),
             pltpu.VMEM((LANES, LANES), jnp.float32),
             pltpu.SemaphoreType.DMA((2,)),
-            pltpu.SemaphoreType.DMA((2, slots)),
-            pltpu.SemaphoreType.DMA((2, slots)),
+            pltpu.SemaphoreType.DMA((2, slots, 2)),
+            pltpu.SemaphoreType.DMA((2, slots, 2)),
             pltpu.SemaphoreType.DMA((group,)),
             pltpu.SemaphoreType.DMA((group,)),
             pltpu.SemaphoreType.DMA((plane,)),

time: 40.8 us -> 40.9 us (level)
  no operation moved by 1% of the time
where the time goes in v3:
time: 40.9 us; the launch traced here: 40.7 us
  Pallas kernels  38.8 us (95%)
  local copies, waits for them, and re-layouts  1.28 us (3%)
  between operations  0.66 us (2%)
    pallas_call x1, Pallas kernels, on_device(): pl.pallas_call(functools.partial(kernel, n_freq, n_depth, scale), out_sha...  38.8 us
    unnamed x1, local copies, waits for them, and re-layouts  1.28 us

profile of v3, /device:TPU:1, one launch (start us, length us, event | category | flops | bytes accessed | tf_op | source)
XLA Modules:
  0.0 40.7 jit_solution(12822452189962453165)
XLA Ops:
  0.7 38.8 %shard_map.64 = f32[4,2,64]{2,1,0:T(2,128)} custom-call(bf16[2,1,384,2,256]{4,3,2,1,0:T(2,128)(2,1)} %source.1, bf16[2,1,128,2,256]{4,3,2,1,0:T(2,128)(2,1)} %receiver.1, s32[1,1024]{1,0:T(1,128)} %bitcast.2, s32[1,1024]{1,0:T(1,128)} %bitcast.3, s32[2]{0:T(128)} %bins.1, f32[1]{0:T(128)S(6)} %copy.8.profile), custom_call_target="tpu_custom_call" | custom-call | tf_op jit(solution)/shard_map/pallas_call | solution.py:293
  39.4 1.3 %copy.9 = f32[4,2,64]{2,1,0:T(2,128)} copy(f32[4,2,64]{2,1,0:T(2,128)} %shard_map.64) | data formatting | bytes 4096
